TPU v7x, 32 devices: a whole 2x2x4 slice. The times are simulated.
32 devices in a mesh: batch: 8 (over z, x), mp: 4 (over y, core).
Axes of the slice: x: 2, y: 2, z: 4, core: 2. Of those that a mesh axis runs over, the one named last changes fastest.
Arguments:
- img_feat: bfloat16 [128, 1536], P('batch'), may hold values from -6 to 6
- txt_feat: bfloat16 [128, 1536], P('batch'), may hold values from -6 to 6
- w_img: bfloat16 [1536, 1152], P('batch', 'mp'), may hold values from -0.15625 to 0.15625
- w_txt: bfloat16 [1536, 1152], P('batch', 'mp'), may hold values from -0.15625 to 0.15625
- pair_index: int32 [128], P('batch'), may hold values from 0 to 127, each once
- log_scale: float32 [1], replicated, may hold values from 2 to 2.6
- bias: float32 [1], replicated, may hold values from -6 to -4
Outputs:
- image_grad: float32 [128, 1152], P('batch', 'mp')
- text_grad: float32 [128, 1152], P(('batch', 'mp'))
Inputs may be any that keep to these rules, and one draw needn't show every extreme that they name: `pair_index`: each text index appears exactly once.
All inputs are finite; a program needn't handle non-finite values.
Results may differ from a plain program's by a relative error of at most 0.0046.
Values may be sent and summed in bfloat16 or wider, within the bound.
A program may use at most 64 MiB of HBM per device.

v0:
```python
import jax
import jax.numpy as jnp
from jax import lax
from jax.sharding import PartitionSpec as P

epsilon = 1e-06


def from_behind(value, axis, steps):
    count = lax.axis_size(axis)
    pairs = [(source, (source + steps) % count) for source in range(count)]
    return lax.ppermute(value, axis, pairs)


def normalize(pre):
    values = pre.astype(jnp.float32)
    norm = lax.rsqrt(jnp.sum(values * values, axis=1, keepdims=True) + epsilon)
    return (values * norm).astype(jnp.bfloat16)


def block_update(image, pairing, scale, offset, text, first):
    count = text.shape[0]
    scores = lax.dot_general(
        image, text, (((1,), (1,)), ((), ())), preferred_element_type=jnp.float32
    )
    logits = scale * scores + offset
    columns = first + jnp.arange(count, dtype=jnp.int32)
    label = jnp.where(pairing[:, None] == columns[None, :], 1.0, -1.0).astype(jnp.float32)
    coef = (-label * jax.nn.sigmoid(-label * logits)).astype(jnp.bfloat16)
    image_term = jnp.dot(coef, text, preferred_element_type=jnp.float32)
    text_term = lax.dot_general(
        coef, image, (((0,), (0,)), ((), ())), preferred_element_type=jnp.float32
    )
    return (image_term, text_term)


def local(img_feat, txt_feat, w_img, w_txt, pair_index, log_scale, bias):
    rows = img_feat.shape[0]
    cycle_size = lax.axis_size("batch")
    group_size = lax.axis_size("mp")
    here = lax.axis_index("batch")
    member = lax.axis_index("mp")
    piece_rows = rows // group_size
    columns_part = w_img.shape[1]
    width = group_size * columns_part
    span = min(cycle_size, 32)
    half = span // 2
    first = jnp.dot(
        img_feat,
        lax.all_gather(w_img, "batch", axis=0, tiled=True),
        preferred_element_type=jnp.float32,
    )
    second = jnp.dot(
        txt_feat,
        lax.all_gather(w_txt, "batch", axis=0, tiled=True),
        preferred_element_type=jnp.float32,
    )
    full_img, full_txt = (
        lax.all_gather(first.astype(jnp.bfloat16), "mp", axis=1, tiled=True),
        lax.all_gather(second.astype(jnp.bfloat16), "mp", axis=1, tiled=True),
    )
    image = normalize(full_img)
    own_start = member * piece_rows
    text = normalize(lax.dynamic_slice_in_dim(full_txt, own_start, piece_rows, 0))
    scale = jnp.exp(log_scale[0])
    offset = bias[0]
    image_total = jnp.zeros((rows, width), jnp.float32)
    start_grads = jnp.zeros((piece_rows, width), jnp.float32)

    def first_row(anchor):
        return anchor * rows + member * piece_rows

    moving = from_behind(text, "batch", -half)

    def turn(step, carry):
        moving, grads, totals = carry
        anchor = (here + half - step) % cycle_size
        image_term, text_term = block_update(
            image, pair_index, scale, offset, moving, first_row(anchor)
        )
        moving = from_behind(moving, "batch", 1)
        grads = from_behind(grads + text_term, "batch", 1)
        return (moving, grads, totals + image_term)

    moving, grads, image_total = lax.fori_loop(0, span, turn, (moving, start_grads, image_total))
    text_total = from_behind(grads, "batch", -half)
    image_part = lax.psum_scatter(image_total, "mp", scatter_dimension=1, tiled=True)
    return (scale * image_part, scale * text_total)


def solution(mesh):
    return jax.shard_map(
        local,
        mesh=mesh,
        in_specs=(
            P("batch", None),
            P("batch", None),
            P("batch", "mp"),
            P("batch", "mp"),
            P("batch"),
            P(),
            P(),
        ),
        out_specs=(P("batch", "mp"), P(("batch", "mp"), None)),
        check_vma=False,
    )
```

profile of v0, /device:TPU:0, one launch (start us, length us, event | category | flops | bytes accessed | tf_op | source)
XLA Modules:
  0.0 181.7 jit_solution(2862626169653061791)
XLA Ops:
  7.2 35.7 %all_gather.12 = bf16[1536,288]{1,0:T(8,128)(2,1)S(1)} all-gather(bf16[192,288]{1,0:T(8,128)(2,1)} %param.12), channel_id=1, replica_groups=mesh['batch'=8,'mp'=4] {'batch'}, dimensions={0}, use_global_device_ids=true | all-gather | bytes 995328 | tf_op jit(solution)/shard_map/all_gather | solution.py:55
  43.0 0.3 fusion.8
  43.2 5.2 %all-gather = bf16[4,288,16]{1,2,0:T(8,128)(2,1)S(1)} all-gather(bf16[1,288,16]{1,2,0:T(8,128)(2,1)S(1)} %fusion.8), channel_id=1, replica_groups=mesh['batch'=8,'mp'=4] {'mp'}, dimensions={0}, use_global_device_ids=true | all-gather | bytes 46080 | tf_op jit(solution)/shard_map/all_gather | solution.py:60
  48.8 35.0 %all_gather.14 = bf16[1536,288]{1,0:T(8,128)(2,1)S(1)} all-gather(bf16[192,288]{1,0:T(8,128)(2,1)S(1)} %copy-done.1), channel_id=1, replica_groups=mesh['batch'=8,'mp'=4] {'batch'}, dimensions={0}, use_global_device_ids=true | all-gather | bytes 995328 | tf_op jit(solution)/shard_map/all_gather | solution.py:50
  83.9 0.3 fusion.9
  84.1 5.2 %all-gather.1 = bf16[4,288,16]{1,2,0:T(8,128)(2,1)S(1)} all-gather(bf16[1,288,16]{1,2,0:T(8,128)(2,1)S(1)} %fusion.9), channel_id=1, replica_groups=mesh['batch'=8,'mp'=4] {'mp'}, dimensions={0}, use_global_device_ids=true | all-gather | bytes 46080 | tf_op jit(solution)/shard_map/all_gather | solution.py:59
  90.5 59.9 %while.20 = (s32[]{:T(128)}, bf16[4,1152]{1,0:T(4,128)(2,1)S(1)}, f32[4,1152]{1,0:T(4,128)S(1)}, f32[16,1152]{1,0:T(8,128)S(1)}, s32[16]{0:T(128)S(1)}, /*index=...) while((s32[]{:T(128)}, bf16[4,1152]{1,0:T(4,128)(2,1)S(1)}, ...), condition=%wide.region_3.4_spmd.clone, body=%wide.region_2.3_spmd.clone.sunk | while | flops 484565 | bytes 406372 | solution.py:85
  90.5 0.5 collective-permute-start
  90.9 0.8 fusion.37
  91.7 0.1 convolution_add_fusion.4
  92.0 0.2 convolution_add_fusion.5
  92.2 4.7 %collective-permute-done = bf16[4,1152]{1,0:T(4,128)(2,1)S(1)} collective-permute-done((bf16[4,1152]{1,0:T(4,128)(2,1)S(1)}, bf16[4,1152]{1,0:T(4,128)(2,1)S(1)}, u32[]{:S(2)}, u32[]{:S(2)}) %collective-permute-start) | collective-permute-done | bytes 9248 | tf_op jit(solution)/shard_map/while/body/eval_jaxpr/ppermute | solution.py:12
  96.9 1.4 collective-permute-done.1
  98.4 0.8 fusion.37
  99.1 0.1 convolution_add_fusion.4
  99.3 0.2 convolution_add_fusion.5
  99.5 5.2 %collective-permute-done = bf16[4,1152]{1,0:T(4,128)(2,1)S(1)} collective-permute-done((bf16[4,1152]{1,0:T(4,128)(2,1)S(1)}, bf16[4,1152]{1,0:T(4,128)(2,1)S(1)}, u32[]{:S(2)}, u32[]{:S(2)}) %collective-permute-start) | collective-permute-done | bytes 9248 | tf_op jit(solution)/shard_map/while/body/eval_jaxpr/ppermute | solution.py:12
  104.7 1.1 collective-permute-done.1
  105.8 0.8 fusion.37
  106.7 0.2 convolution_add_fusion.5
  106.9 5.2 %collective-permute-done = bf16[4,1152]{1,0:T(4,128)(2,1)S(1)} collective-permute-done((bf16[4,1152]{1,0:T(4,128)(2,1)S(1)}, bf16[4,1152]{1,0:T(4,128)(2,1)S(1)}, u32[]{:S(2)}, u32[]{:S(2)}) %collective-permute-start) | collective-permute-done | bytes 9248 | tf_op jit(solution)/shard_map/while/body/eval_jaxpr/ppermute | solution.py:12
  112.1 1.1 collective-permute-done.1
  113.2 0.8 fusion.37
  114.2 0.2 convolution_add_fusion.5
  114.4 5.2 %collective-permute-done = bf16[4,1152]{1,0:T(4,128)(2,1)S(1)} collective-permute-done((bf16[4,1152]{1,0:T(4,128)(2,1)S(1)}, bf16[4,1152]{1,0:T(4,128)(2,1)S(1)}, u32[]{:S(2)}, u32[]{:S(2)}) %collective-permute-start) | collective-permute-done | bytes 9248 | tf_op jit(solution)/shard_map/while/body/eval_jaxpr/ppermute | solution.py:12
  119.5 1.1 collective-permute-done.1
  120.7 0.8 fusion.37
  121.6 0.2 convolution_add_fusion.5
  121.8 5.2 %collective-permute-done = bf16[4,1152]{1,0:T(4,128)(2,1)S(1)} collective-permute-done((bf16[4,1152]{1,0:T(4,128)(2,1)S(1)}, bf16[4,1152]{1,0:T(4,128)(2,1)S(1)}, u32[]{:S(2)}, u32[]{:S(2)}) %collective-permute-start) | collective-permute-done | bytes 9248 | tf_op jit(solution)/shard_map/while/body/eval_jaxpr/ppermute | solution.py:12
  127.0 1.1 collective-permute-done.1
  128.1 0.8 fusion.37
  129.0 0.2 convolution_add_fusion.5
  129.2 5.2 %collective-permute-done = bf16[4,1152]{1,0:T(4,128)(2,1)S(1)} collective-permute-done((bf16[4,1152]{1,0:T(4,128)(2,1)S(1)}, bf16[4,1152]{1,0:T(4,128)(2,1)S(1)}, u32[]{:S(2)}, u32[]{:S(2)}) %collective-permute-start) | collective-permute-done | bytes 9248 | tf_op jit(solution)/shard_map/while/body/eval_jaxpr/ppermute | solution.py:12
  134.4 1.1 collective-permute-done.1
  135.5 0.8 fusion.37
  136.4 0.2 convolution_add_fusion.5
  136.7 5.3 %collective-permute-done = bf16[4,1152]{1,0:T(4,128)(2,1)S(1)} collective-permute-done((bf16[4,1152]{1,0:T(4,128)(2,1)S(1)}, bf16[4,1152]{1,0:T(4,128)(2,1)S(1)}, u32[]{:S(2)}, u32[]{:S(2)}) %collective-permute-start) | collective-permute-done | bytes 9248 | tf_op jit(solution)/shard_map/while/body/eval_jaxpr/ppermute | solution.py:12
  141.9 1.0 collective-permute-done.1
  143.0 0.8 fusion.37
  143.9 0.2 convolution_add_fusion.5
  144.1 5.2 %collective-permute-done = bf16[4,1152]{1,0:T(4,128)(2,1)S(1)} collective-permute-done((bf16[4,1152]{1,0:T(4,128)(2,1)S(1)}, bf16[4,1152]{1,0:T(4,128)(2,1)S(1)}, u32[]{:S(2)}, u32[]{:S(2)}) %collective-permute-start) | collective-permute-done | bytes 9248 | tf_op jit(solution)/shard_map/while/body/eval_jaxpr/ppermute | solution.py:12
  149.3 1.1 collective-permute-done.1
  150.3 1.1 copy.13
  151.4 3.6 %collective-permute-done.3 = f32[4,1152]{1,0:T(4,128)S(1)} collective-permute-done((f32[4,1152]{1,0:T(4,128)S(1)}, f32[4,1152]{1,0:T(4,128)S(1)}, u32[]{:S(2)}, u32[]{:S(2)}) %collective-permute-start.3) | collective-permute-done | bytes 18464 | tf_op jit(solution)/shard_map/ppermute | solution.py:12
  155.0 0.6 broadcast_multiply_fusion.1
  155.6 17.7 %reduce-scatter.4.cloned.1.call-done = f32[288,16]{1,0:T(8,128)} async-done(((f32[1152,16]{1,0:T(8,128)}), f32[288,16]{1,0:T(8,128)}) %reduce-scatter.4.cloned.1.call-update) | async-done | bytes 18448
  173.3 1.0 copy.14
  174.3 0.6 broadcast_multiply_fusion
  (62 shorter events, 1.8 us)
Async XLA Ops:
  7.2 35.8 %copy-start = (bf16[16,1536]{1,0:T(8,128)(2,1)S(1)}, bf16[16,1536]{1,0:T(8,128)(2,1)}, u32[]{:S(2)}) copy-start(bf16[16,1536]{1,0:T(8,128)(2,1)} %param.10) | copy-start | bytes 147460
  7.2 166.1 %reduce-scatter.4.cloned.1.call-start = ((), (), s32[]{:S(2)}) async-start(), calls=%async_computation.1 | async-start | bytes 737280
  7.2 41.6 %copy-start.1 = (bf16[192,288]{1,0:T(8,128)(2,1)S(1)}, bf16[192,288]{1,0:T(8,128)(2,1)}, u32[]{:S(2)}) copy-start(bf16[192,288]{1,0:T(8,128)(2,1)} %param.11) | copy-start | bytes 331780
  42.9 40.9 %copy-start.2 = (bf16[16,1536]{1,0:T(8,128)(2,1)S(1)}, bf16[16,1536]{1,0:T(8,128)(2,1)}, u32[]{:S(2)}) copy-start(bf16[16,1536]{1,0:T(8,128)(2,1)} %param.9) | copy-start | bytes 147460
  48.8 41.6 %collective-permute-start.2 = (bf16[4,1152]{1,0:T(4,128)(2,1)S(1)}, bf16[4,1152]{1,0:T(4,128)(2,1)S(1)}, u32[]{:S(2)}, u32[]{:S(2)}) collective-permute-start(bf16[4,1152]{1,0:T(4,128)(2,1)S(1)} %fusion.13), channel_id=1, source_target_pairs={{0,16},{4,20},{8,24},{12,28},{16,0},{20,4},{24,8},{28,12},{1,17},{... | collective-permute-start | bytes 27656 | tf_op jit(solution)/shard_map/ppermute | solution.py:12
  83.9 6.6 %copy-start.3 = (s32[16]{0:T(128)S(1)}, s32[16]{0:T(128)}, u32[]{:S(2)}) copy-start(s32[16]{0:T(128)} %param.13) | copy-start | bytes 196
  90.5 6.4 %collective-permute-start = (bf16[4,1152]{1,0:T(4,128)(2,1)S(1)}, bf16[4,1152]{1,0:T(4,128)(2,1)S(1)}, u32[]{:S(2)}, u32[]{:S(2)}) collective-permute-start(bf16[4,1152]{1,0:T(4,128)(2,1)S(1)} %copy.20), channel_id=1, source_target_pairs={{0,4},{4,8},{8,12},{12,16},{16,20},{20,24},{24,28},{28,0},{1,5},{5... | collective-permute-start | bytes 27656 | tf_op jit(solution)/shard_map/while/body/eval_jaxpr/ppermute | solution.py:12
  91.9 6.5 %collective-permute-start.1 = (f32[4,1152]{1,0:T(4,128)S(1)}, f32[4,1152]{1,0:T(4,128)S(1)}, u32[]{:S(2)}, u32[]{:S(2)}) collective-permute-start(f32[4,1152]{1,0:T(4,128)S(1)} %convolution_add_fusion.4), channel_id=1, source_target_pairs={{0,4},{4,8},{8,12},{12,16},{16,20},{20,24},{24,28},{28,0},{1,5},{5... | collective-permute-start | bytes 55304 | tf_op jit(solution)/shard_map/while/body/eval_jaxpr/ppermute | solution.py:12
  98.3 6.4 %collective-permute-start = (bf16[4,1152]{1,0:T(4,128)(2,1)S(1)}, bf16[4,1152]{1,0:T(4,128)(2,1)S(1)}, u32[]{:S(2)}, u32[]{:S(2)}) collective-permute-start(bf16[4,1152]{1,0:T(4,128)(2,1)S(1)} %copy.20), channel_id=1, source_target_pairs={{0,4},{4,8},{8,12},{12,16},{16,20},{20,24},{24,28},{28,0},{1,5},{5... | collective-permute-start | bytes 27656 | tf_op jit(solution)/shard_map/while/body/eval_jaxpr/ppermute | solution.py:12
  99.3 6.5 %collective-permute-start.1 = (f32[4,1152]{1,0:T(4,128)S(1)}, f32[4,1152]{1,0:T(4,128)S(1)}, u32[]{:S(2)}, u32[]{:S(2)}) collective-permute-start(f32[4,1152]{1,0:T(4,128)S(1)} %convolution_add_fusion.4), channel_id=1, source_target_pairs={{0,4},{4,8},{8,12},{12,16},{16,20},{20,24},{24,28},{28,0},{1,5},{5... | collective-permute-start | bytes 55304 | tf_op jit(solution)/shard_map/while/body/eval_jaxpr/ppermute | solution.py:12
  105.8 6.4 %collective-permute-start = (bf16[4,1152]{1,0:T(4,128)(2,1)S(1)}, bf16[4,1152]{1,0:T(4,128)(2,1)S(1)}, u32[]{:S(2)}, u32[]{:S(2)}) collective-permute-start(bf16[4,1152]{1,0:T(4,128)(2,1)S(1)} %copy.20), channel_id=1, source_target_pairs={{0,4},{4,8},{8,12},{12,16},{16,20},{20,24},{24,28},{28,0},{1,5},{5... | collective-permute-start | bytes 27656 | tf_op jit(solution)/shard_map/while/body/eval_jaxpr/ppermute | solution.py:12
  106.7 6.5 %collective-permute-start.1 = (f32[4,1152]{1,0:T(4,128)S(1)}, f32[4,1152]{1,0:T(4,128)S(1)}, u32[]{:S(2)}, u32[]{:S(2)}) collective-permute-start(f32[4,1152]{1,0:T(4,128)S(1)} %convolution_add_fusion.4), channel_id=1, source_target_pairs={{0,4},{4,8},{8,12},{12,16},{16,20},{20,24},{24,28},{28,0},{1,5},{5... | collective-permute-start | bytes 55304 | tf_op jit(solution)/shard_map/while/body/eval_jaxpr/ppermute | solution.py:12
  113.2 6.4 %collective-permute-start = (bf16[4,1152]{1,0:T(4,128)(2,1)S(1)}, bf16[4,1152]{1,0:T(4,128)(2,1)S(1)}, u32[]{:S(2)}, u32[]{:S(2)}) collective-permute-start(bf16[4,1152]{1,0:T(4,128)(2,1)S(1)} %copy.20), channel_id=1, source_target_pairs={{0,4},{4,8},{8,12},{12,16},{16,20},{20,24},{24,28},{28,0},{1,5},{5... | collective-permute-start | bytes 27656 | tf_op jit(solution)/shard_map/while/body/eval_jaxpr/ppermute | solution.py:12
  114.1 6.5 %collective-permute-start.1 = (f32[4,1152]{1,0:T(4,128)S(1)}, f32[4,1152]{1,0:T(4,128)S(1)}, u32[]{:S(2)}, u32[]{:S(2)}) collective-permute-start(f32[4,1152]{1,0:T(4,128)S(1)} %convolution_add_fusion.4), channel_id=1, source_target_pairs={{0,4},{4,8},{8,12},{12,16},{16,20},{20,24},{24,28},{28,0},{1,5},{5... | collective-permute-start | bytes 55304 | tf_op jit(solution)/shard_map/while/body/eval_jaxpr/ppermute | solution.py:12
  120.6 6.4 %collective-permute-start = (bf16[4,1152]{1,0:T(4,128)(2,1)S(1)}, bf16[4,1152]{1,0:T(4,128)(2,1)S(1)}, u32[]{:S(2)}, u32[]{:S(2)}) collective-permute-start(bf16[4,1152]{1,0:T(4,128)(2,1)S(1)} %copy.20), channel_id=1, source_target_pairs={{0,4},{4,8},{8,12},{12,16},{16,20},{20,24},{24,28},{28,0},{1,5},{5... | collective-permute-start | bytes 27656 | tf_op jit(solution)/shard_map/while/body/eval_jaxpr/ppermute | solution.py:12
  121.6 6.5 %collective-permute-start.1 = (f32[4,1152]{1,0:T(4,128)S(1)}, f32[4,1152]{1,0:T(4,128)S(1)}, u32[]{:S(2)}, u32[]{:S(2)}) collective-permute-start(f32[4,1152]{1,0:T(4,128)S(1)} %convolution_add_fusion.4), channel_id=1, source_target_pairs={{0,4},{4,8},{8,12},{12,16},{16,20},{20,24},{24,28},{28,0},{1,5},{5... | collective-permute-start | bytes 55304 | tf_op jit(solution)/shard_map/while/body/eval_jaxpr/ppermute | solution.py:12
  128.1 6.4 %collective-permute-start = (bf16[4,1152]{1,0:T(4,128)(2,1)S(1)}, bf16[4,1152]{1,0:T(4,128)(2,1)S(1)}, u32[]{:S(2)}, u32[]{:S(2)}) collective-permute-start(bf16[4,1152]{1,0:T(4,128)(2,1)S(1)} %copy.20), channel_id=1, source_target_pairs={{0,4},{4,8},{8,12},{12,16},{16,20},{20,24},{24,28},{28,0},{1,5},{5... | collective-permute-start | bytes 27656 | tf_op jit(solution)/shard_map/while/body/eval_jaxpr/ppermute | solution.py:12
  129.0 6.5 %collective-permute-start.1 = (f32[4,1152]{1,0:T(4,128)S(1)}, f32[4,1152]{1,0:T(4,128)S(1)}, u32[]{:S(2)}, u32[]{:S(2)}) collective-permute-start(f32[4,1152]{1,0:T(4,128)S(1)} %convolution_add_fusion.4), channel_id=1, source_target_pairs={{0,4},{4,8},{8,12},{12,16},{16,20},{20,24},{24,28},{28,0},{1,5},{5... | collective-permute-start | bytes 55304 | tf_op jit(solution)/shard_map/while/body/eval_jaxpr/ppermute | solution.py:12
  135.5 6.5 %collective-permute-start = (bf16[4,1152]{1,0:T(4,128)(2,1)S(1)}, bf16[4,1152]{1,0:T(4,128)(2,1)S(1)}, u32[]{:S(2)}, u32[]{:S(2)}) collective-permute-start(bf16[4,1152]{1,0:T(4,128)(2,1)S(1)} %copy.20), channel_id=1, source_target_pairs={{0,4},{4,8},{8,12},{12,16},{16,20},{20,24},{24,28},{28,0},{1,5},{5... | collective-permute-start | bytes 27656 | tf_op jit(solution)/shard_map/while/body/eval_jaxpr/ppermute | solution.py:12
  136.4 6.5 %collective-permute-start.1 = (f32[4,1152]{1,0:T(4,128)S(1)}, f32[4,1152]{1,0:T(4,128)S(1)}, u32[]{:S(2)}, u32[]{:S(2)}) collective-permute-start(f32[4,1152]{1,0:T(4,128)S(1)} %convolution_add_fusion.4), channel_id=1, source_target_pairs={{0,4},{4,8},{8,12},{12,16},{16,20},{20,24},{24,28},{28,0},{1,5},{5... | collective-permute-start | bytes 55304 | tf_op jit(solution)/shard_map/while/body/eval_jaxpr/ppermute | solution.py:12
  142.9 6.4 %collective-permute-start = (bf16[4,1152]{1,0:T(4,128)(2,1)S(1)}, bf16[4,1152]{1,0:T(4,128)(2,1)S(1)}, u32[]{:S(2)}, u32[]{:S(2)}) collective-permute-start(bf16[4,1152]{1,0:T(4,128)(2,1)S(1)} %copy.20), channel_id=1, source_target_pairs={{0,4},{4,8},{8,12},{12,16},{16,20},{20,24},{24,28},{28,0},{1,5},{5... | collective-permute-start | bytes 27656 | tf_op jit(solution)/shard_map/while/body/eval_jaxpr/ppermute | solution.py:12
  143.9 6.5 %collective-permute-start.1 = (f32[4,1152]{1,0:T(4,128)S(1)}, f32[4,1152]{1,0:T(4,128)S(1)}, u32[]{:S(2)}, u32[]{:S(2)}) collective-permute-start(f32[4,1152]{1,0:T(4,128)S(1)} %convolution_add_fusion.4), channel_id=1, source_target_pairs={{0,4},{4,8},{8,12},{12,16},{16,20},{20,24},{24,28},{28,0},{1,5},{5... | collective-permute-start | bytes 55304 | tf_op jit(solution)/shard_map/while/body/eval_jaxpr/ppermute | solution.py:12
  150.3 4.7 %collective-permute-start.3 = (f32[4,1152]{1,0:T(4,128)S(1)}, f32[4,1152]{1,0:T(4,128)S(1)}, u32[]{:S(2)}, u32[]{:S(2)}) collective-permute-start(f32[4,1152]{1,0:T(4,128)S(1)} %get-tuple-element.251), channel_id=1, source_target_pairs={{0,16},{4,20},{8,24},{12,28},{16,0},{20,4},{24,8},{28,12},{1,17},{... | collective-permute-start | bytes 55304 | tf_op jit(solution)/shard_map/ppermute | solution.py:12
Sparse Core Ops, SparseCore 0:
  151.5 21.6 reduce-scatter.3
where the time goes:
time: 182 us
  blocking collectives  81.2 us (45%)
  waiting for transfers between devices  71.1 us (39%)
  between operations  14.8 us (8%)
  matrix products  9.47 us (5%)
  local copies, waits for them, and re-layouts  2.37 us (1%)
    ppermute x18, waiting for transfers between devices, from_behind(): return lax.ppermute(value, axis, pairs)  53.4 us
    all_gather x1, blocking collectives, local(): lax.all_gather(w_txt, 'batch', axis=0, tiled=True)  35.7 us
    all_gather x1, blocking collectives, local(): lax.all_gather(w_img, 'batch', axis=0, tiled=True)  35 us
    unnamed x2, waiting for transfers between devices  17.7 us
    dot_general x8, matrix products, block_update(): lax.dot_general(image, text, (((1,), (1,)), ((), ())), preferred_element_...  6.23 us
    all_gather x1, blocking collectives, local(): lax.all_gather(first.astype(jnp.bfloat16), 'mp', axis=1, tiled=True)  5.22 us
    all_gather x1, blocking collectives, local(): lax.all_gather(second.astype(jnp.bfloat16), 'mp', axis=1, tiled=True)  5.22 us
  transfers between devices with their start and end apart: 19, of which 18 were waited for; matrix products, arithmetic and copies ran while one was open for 6% of the time, Pallas kernels for 0%

commit v1 on v0

--- a/solution.py
+++ b/solution.py
@@ -1,6 +1,10 @@
+import functools
+
 import jax
 import jax.numpy as jnp
 from jax import lax
+from jax.experimental import pallas as pl
+from jax.experimental.pallas import tpu as pltpu
 from jax.sharding import PartitionSpec as P
 
 epsilon = 1e-06
@@ -34,7 +38,7 @@
     return (image_term, text_term)
 
 
-def local(img_feat, txt_feat, w_img, w_txt, pair_index, log_scale, bias):
+def windowed(img_feat, txt_feat, w_img, w_txt, pair_index, log_scale, bias):
     rows = img_feat.shape[0]
     cycle_size = lax.axis_size("batch")
     group_size = lax.axis_size("mp")
@@ -86,6 +90,202 @@
     text_total = from_behind(grads, "batch", -half)
     image_part = lax.psum_scatter(image_total, "mp", scatter_dimension=1, tiled=True)
     return (scale * image_part, scale * text_total)
+
+
+MESH = pl.DeviceIdType.MESH
+
+
+def coefficients(scores, matched, scale, offset):
+    label = jnp.where(matched, 1.0, -1.0).astype(jnp.float32)
+    logits = scale * scores + offset
+    return (-label * jax.nn.sigmoid(-label * logits)).astype(jnp.bfloat16)
+
+
+def full_window_kernel(
+    cycle, group, feat, w_img, w_txt, pair, log_scale, bias, image_out, text_out,
+    feats, partial, parts, every, squares, scores, pairs, pieces,
+    feat_send, feat_recv, part_send, part_recv, every_send, every_recv,
+    square_send, square_recv, score_send, score_recv, pair_send, pair_recv,
+    piece_send, piece_recv,
+):
+    here = lax.axis_index("batch")
+    member = lax.axis_index("mp")
+    rows = pair.shape[0]
+    total = cycle * rows
+    columns = w_img.shape[1]
+    piece_rows = rows // group
+
+    def ahead(d):
+        return lax.rem(here + d, cycle)
+
+    def behind(d):
+        return lax.rem(here + cycle - d, cycle)
+
+    def mate(e):
+        return lax.rem(member + e, group)
+
+    def mate_behind(e):
+        return lax.rem(member + group - e, group)
+
+    def copy(src, dst, send, recv, device):
+        return pltpu.make_async_remote_copy(
+            src_ref=src, dst_ref=dst, send_sem=send, recv_sem=recv,
+            device_id=device, device_id_type=MESH,
+        )
+
+    barrier = pltpu.get_barrier_semaphore()
+    for d in range(1, cycle):
+        pl.semaphore_signal(barrier, inc=1, device_id=(ahead(d), member), device_id_type=MESH)
+    for e in range(1, group):
+        pl.semaphore_signal(barrier, inc=1, device_id=(here, mate(e)), device_id_type=MESH)
+
+    lane = lax.broadcasted_iota(jnp.int32, (rows, total), 1)
+    row = lax.broadcasted_iota(jnp.int32, (rows, total), 0)
+    own_pair = jnp.broadcast_to(pair[...], (rows, total))
+    spread = jnp.where(lane - here * rows == row, own_pair.astype(jnp.float32), 0.0)
+    pairs[here] = jnp.broadcast_to(jnp.sum(spread, axis=0, keepdims=True), (8, total))
+    pl.semaphore_wait(barrier, cycle + group - 2)
+
+    sends = []
+    for d in range(1, cycle):
+        c = copy(feat.at[ahead(d)], feats.at[here], feat_send.at[d], feat_recv.at[d], (ahead(d), member))
+        c.start()
+        sends.append(c)
+    for d in range(1, cycle):
+        c = copy(pairs.at[here], pairs.at[here], pair_send.at[d], pair_recv.at[d], (ahead(d), member))
+        c.start()
+        sends.append(c)
+
+    def product(block):
+        return (
+            jnp.dot(block[:rows], w_img[...], preferred_element_type=jnp.float32),
+            jnp.dot(block[rows:], w_txt[...], preferred_element_type=jnp.float32),
+        )
+
+    image_sum, text_sum = product(feat[here])
+    for d in range(1, cycle):
+        source = behind(d)
+        copy(feat.at[here], feats.at[source], feat_send.at[d], feat_recv.at[d], (source, member)).wait_recv()
+        first, second = product(feats[source])
+        partial[source, :rows] = first.astype(jnp.bfloat16)
+        partial[source, rows:] = second.astype(jnp.bfloat16)
+        c = copy(partial.at[source], parts.at[here], part_send.at[d], part_recv.at[d], (source, member))
+        c.start()
+        sends.append(c)
+    for d in range(1, cycle):
+        source = ahead(d)
+        copy(partial.at[source], parts.at[source], part_send.at[d], part_recv.at[d], (source, member)).wait_recv()
+        image_sum = image_sum + parts[source, :rows].astype(jnp.float32)
+        text_sum = text_sum + parts[source, rows:].astype(jnp.float32)
+
+    pre = jnp.concatenate([image_sum, text_sum], axis=0).astype(jnp.bfloat16).astype(jnp.float32)
+    squares[member] = jnp.broadcast_to(jnp.sum(pre * pre, axis=1, keepdims=True), (2 * rows, 128))
+    for e in range(1, group):
+        c = copy(squares.at[member], squares.at[member], square_send.at[e], square_recv.at[e], (here, mate(e)))
+        c.start()
+        sends.append(c)
+    for e in range(1, group):
+        source = mate_behind(e)
+        copy(squares.at[source], squares.at[source], square_send.at[e], square_recv.at[e], (here, source)).wait_recv()
+    square = squares[0]
+    for k in range(1, group):
+        square = square + squares[k]
+    norm = lax.rsqrt(square + epsilon)[:, :1]
+    own = (pre * norm).astype(jnp.bfloat16)
+    every[here] = own
+    for d in range(1, cycle):
+        c = copy(every.at[here], every.at[here], every_send.at[d], every_recv.at[d], (ahead(d), member))
+        c.start()
+        sends.append(c)
+    for d in range(1, cycle):
+        source = behind(d)
+        copy(every.at[source], every.at[source], every_send.at[d], every_recv.at[d], (source, member)).wait_recv()
+        copy(pairs.at[source], pairs.at[source], pair_send.at[d], pair_recv.at[d], (source, member)).wait_recv()
+    images = every[:, :rows].reshape(total, columns)
+    texts = every[:, rows:].reshape(total, columns)
+    across = (((1,), (1,)), ((), ()))
+    scores[member, :rows] = lax.dot_general(own[:rows], texts, across, preferred_element_type=jnp.float32)
+    scores[member, rows:] = lax.dot_general(own[rows:], images, across, preferred_element_type=jnp.float32)
+    for e in range(1, group):
+        c = copy(scores.at[member], scores.at[member], score_send.at[e], score_recv.at[e], (here, mate(e)))
+        c.start()
+        sends.append(c)
+    scale = jnp.exp(jnp.full((1, 1), log_scale[0], jnp.float32))
+    offset = bias[0]
+    all_pairs = pairs[0]
+    for k in range(1, cycle):
+        all_pairs = all_pairs + pairs[k]
+    of_texts = jnp.broadcast_to(all_pairs[:1], (rows, total)) == (here * rows + row).astype(jnp.float32)
+    of_images = own_pair == lane
+    for e in range(1, group):
+        source = mate_behind(e)
+        copy(scores.at[source], scores.at[source], score_send.at[e], score_recv.at[e], (here, source)).wait_recv()
+    score = scores[0]
+    for k in range(1, group):
+        score = score + scores[k]
+    text_coef = coefficients(score[rows:], of_texts, scale, offset)
+    text_grad = scale * jnp.dot(text_coef, images, preferred_element_type=jnp.float32)
+    for k in range(group):
+        pieces[0, k] = text_grad[k * piece_rows:(k + 1) * piece_rows]
+    for e in range(1, group):
+        c = copy(pieces.at[0, mate(e)], pieces.at[1, member], piece_send.at[e], piece_recv.at[e], (here, mate(e)))
+        c.start()
+        sends.append(c)
+    pieces[1, member] = pieces[0, member]
+    image_coef = coefficients(score[:rows], of_images, scale, offset)
+    image_out[...] = scale * jnp.dot(image_coef, texts, preferred_element_type=jnp.float32)
+    for e in range(1, group):
+        source = mate_behind(e)
+        copy(pieces.at[0, source], pieces.at[1, source], piece_send.at[e], piece_recv.at[e], (here, source)).wait_recv()
+    for k in range(group):
+        text_out[:, k * columns:(k + 1) * columns] = pieces[1, k]
+    for c in sends:
+        c.wait_send()
+
+
+def full_window(img_feat, txt_feat, w_img, w_txt, pair_index, log_scale, bias):
+    cycle = lax.axis_size("batch")
+    group = lax.axis_size("mp")
+    rows = img_feat.shape[0]
+    depth, columns = w_img.shape
+    total = cycle * rows
+    feat = jnp.concatenate([img_feat, txt_feat], axis=0)
+    feat = feat.reshape(2 * rows, cycle, depth).transpose(1, 0, 2)
+    vmem = pl.BlockSpec(memory_space=pltpu.VMEM)
+    smem = pl.BlockSpec(memory_space=pltpu.SMEM)
+    batch_sems = [pltpu.SemaphoreType.DMA((cycle,))] * 2
+    group_sems = [pltpu.SemaphoreType.DMA((group,))] * 2
+    return pl.pallas_call(
+        functools.partial(full_window_kernel, cycle, group),
+        out_shape=(
+            jax.ShapeDtypeStruct((rows, columns), jnp.float32),
+            jax.ShapeDtypeStruct((rows // group, group * columns), jnp.float32),
+        ),
+        in_specs=[vmem, vmem, vmem, vmem, smem, smem],
+        out_specs=(vmem, vmem),
+        scratch_shapes=[
+            pltpu.VMEM((cycle, 2 * rows, depth), jnp.bfloat16),
+            pltpu.VMEM((cycle, 2 * rows, columns), jnp.bfloat16),
+            pltpu.VMEM((cycle, 2 * rows, columns), jnp.bfloat16),
+            pltpu.VMEM((cycle, 2 * rows, columns), jnp.bfloat16),
+            pltpu.VMEM((group, 2 * rows, 128), jnp.float32),
+            pltpu.VMEM((group, 2 * rows, total), jnp.float32),
+            pltpu.VMEM((cycle, 8, total), jnp.float32),
+            pltpu.VMEM((2, group, rows // group, columns), jnp.float32),
+        ]
+        + batch_sems * 3
+        + group_sems * 2
+        + batch_sems
+        + group_sems,
+        compiler_params=pltpu.CompilerParams(collective_id=0, has_side_effects=True),
+    )(feat, w_img, w_txt, pair_index.reshape(rows, 1), log_scale, bias)
+
+
+def local(*operands):
+    cycle = lax.axis_size("batch")
+    if min(cycle, 32) == cycle:
+        return full_window(*operands)
+    return windowed(*operands)
 
 
 def solution(mesh):

time: 182 us -> 39.8 us (0.22)
  blocking collectives: 81.2 us -> 0 us
  waiting for transfers between devices: 71.1 us -> 0 us
  Pallas kernels: 0 us -> 32.3 us
  between operations: 14.8 us -> 1.96 us
  matrix products: 9.47 us -> 0 us
    all_gather x4 -> x0, blocking collectives: 81.2 us -> none  [the longest x1 35.7 us: local(): lax.all_gather(w_txt, 'batch', axis=0, tiled=True)]
    ppermute x18 -> x0, waiting for transfers between devices: 53.4 us -> none  [from_behind(): return lax.ppermute(value, axis, pairs)]
    pallas_call x0 -> x1, Pallas kernels: none -> 32.3 us  [full_window(): pl.pallas_call(functools.partial(full_window_kernel, cycle, group), out_s...]
    unnamed x2 -> x0, waiting for transfers between devices: 17.7 us -> none
    dot_general x26 -> x0, matrix products: 9.47 us -> none  [the longest x8 6.23 us: block_update(): lax.dot_general(image, text, (((1,), (1,)), ((), ())), preferred_element_...]
  transfers between devices with their start and end apart: 19 -> 0, of which waited for: 18 -> 0; matrix products, arithmetic and copies ran while one was open for 6% -> 0% of each run, Pallas kernels for 0% -> 0%
where the time goes in v1:
time: 39.8 us; the launch traced here: 39.2 us
  Pallas kernels  32.3 us (81%)
  local copies, waits for them, and re-layouts  4.12 us (10%)
  between operations  1.96 us (5%)
  other arithmetic  0.83 us (2%)
    pallas_call x1, Pallas kernels, full_window(): pl.pallas_call(functools.partial(full_window_kernel, cycle, group), out_s...  32.3 us
    unnamed x6, local copies, waits for them, and re-layouts  2.62 us
    concatenate x1, other arithmetic, full_window(): feat = jnp.concatenate([img_feat, txt_feat], axis=0)  0.83 us
    reshape x2, local copies, waits for them, and re-layouts, full_window(): feat = feat.reshape(2 * rows, cycle, depth).transpose(1, 0, 2)  0.83 us

profile of v1, /device:TPU:0, one launch (start us, length us, event | category | flops | bytes accessed | tf_op | source)
XLA Modules:
  0.0 39.2 jit_solution(3800275603012342839)
XLA Ops:
  0.6 0.8 %pad_maximum_fusion = bf16[32,1536]{1,0:T(8,128)(2,1)S(1)} fusion(bf16[16,1536]{1,0:T(8,128)(2,1)} %param.8, bf16[16,1536]{1,0:T(8,128)(2,1)} %param.7), kind=kLoop, calls=%fused_computation.1 | loop fusion | flops 196608 | bytes 196608 | tf_op jit(solution)/shard_map/concatenate | solution.py:252
  1.5 0.2 reshape.10
  1.6 0.7 %copy.13 = bf16[32,8,192]{2,0,1:T(8,128)(2,1)} copy(bf16[32,8,192]{2,1,0:T(8,128)(2,1)S(1)} %reshape.10) | data formatting | bytes 196608 | tf_op jit(solution)/shard_map/reshape | solution.py:253
  2.3 0.0 copy-start.1
  2.3 0.7 %copy-done.1 = s32[16]{0:T(128)S(1)} copy-done((s32[16]{0:T(128)S(1)}, s32[16]{0:T(128)}, u32[]{:S(2)}) %copy-start.1) | copy-done | bytes 88
  3.0 0.7 %copy.11.pair = s32[16,1]{1,0:T(8,128)} copy(s32[16,1]{0,1:T(1,128)S(1)} %bitcast.5) | data formatting | bytes 128 | tf_op jit(solution)/shard_map/reshape | solution.py:281
  4.9 32.3 %shard_map.86 = (f32[16,288]{1,0:T(8,128)}, f32[4,1152]{1,0:T(4,128)}) custom-call(bf16[8,32,192]{2,1,0:T(8,128)(2,1)} %bitcast.4, bf16[192,288]{1,0:T(8,128)(2,1)} %w_img.1, bf16[192,288]{1,0:T(8,128)(2,1)} %w_txt.1, s32[16,1]{1,0:T(8,128)} %copy.11.pair, f32[1]{0:T(128)S(6)} %copy.16.log_scale, f32[1]{0:T(128)S(6)} %copy.17.bias), custom_call_target="tpu_custom_call" | custom-call | tf_op jit(solution)/shard_map/pallas_call | solution.py:258
  37.2 0.0 copy-start
  37.2 1.4 %copy.18 = f32[16,288]{1,0:T(8,128)} copy(f32[16,288]{1,0:T(8,128)} %get-tuple-element.4) | data formatting | bytes 36864
  38.6 0.0 copy-done
  38.6 0.6 %copy.19 = f32[4,1152]{1,0:T(4,128)} copy(f32[4,1152]{1,0:T(4,128)S(1)} %copy-done) | data formatting | bytes 36864
Async XLA Ops:
  2.3 0.7 %copy-start.1 = (s32[16]{0:T(128)S(1)}, s32[16]{0:T(128)}, u32[]{:S(2)}) copy-start(s32[16]{0:T(128)} %param.11) | copy-start | bytes 196
  37.2 1.4 %copy-start = (f32[4,1152]{1,0:T(4,128)S(1)}, f32[4,1152]{1,0:T(4,128)}, u32[]{:S(2)}) copy-start(f32[4,1152]{1,0:T(4,128)} %get-tuple-element.5) | copy-start | bytes 55300

commit v2 on v1

--- a/solution.py
+++ b/solution.py
@@ -98,21 +98,33 @@
 def coefficients(scores, matched, scale, offset):
     label = jnp.where(matched, 1.0, -1.0).astype(jnp.float32)
     logits = scale * scores + offset
-    return (-label * jax.nn.sigmoid(-label * logits)).astype(jnp.bfloat16)
+    return (-label * jax.nn.sigmoid(-label * logits)).astype(jnp.bfloat16).astype(jnp.float32)
+
+
+def weighted(coef, block):
+    high = coef.astype(jnp.bfloat16)
+    low = (coef - high.astype(jnp.float32)).astype(jnp.bfloat16)
+    both = jnp.dot(jnp.concatenate([high, low], axis=0), block, preferred_element_type=jnp.float32)
+    return both[: coef.shape[0]] + both[coef.shape[0] :]
+
+
+def cover(depth):
+    return -(-depth // 128) * 128
 
 
 def full_window_kernel(
-    cycle, group, feat, w_img, w_txt, pair, log_scale, bias, image_out, text_out,
-    feats, partial, parts, every, squares, scores, pairs, pieces,
-    feat_send, feat_recv, part_send, part_recv, every_send, every_recv,
-    square_send, square_recv, score_send, score_recv, pair_send, pair_recv,
-    piece_send, piece_recv,
+    cycle, group, img_feat, txt_feat, w_img, w_txt, pair, log_scale, bias, image_out, text_out,
+    feat, weight, own_index, own_scale, own_bias, feats, partial, parts, every, squares, scores, norms, pieces,
+    stage, feat_send, feat_recv, part_send, part_recv, every_send, every_recv,
+    norm_send, norm_recv, square_send, square_recv, score_send, score_recv, piece_send, piece_recv,
 ):
     here = lax.axis_index("batch")
     member = lax.axis_index("mp")
-    rows = pair.shape[0]
+    rows = img_feat.shape[0]
     total = cycle * rows
-    columns = w_img.shape[1]
+    depth, columns = w_img.shape
+    width = weight.shape[1]
+    spare = width - depth
     piece_rows = rows // group
 
     def ahead(d):
@@ -139,33 +151,57 @@
     for e in range(1, group):
         pl.semaphore_signal(barrier, inc=1, device_id=(here, mate(e)), device_id_type=MESH)
 
+    shift = lax.rem(here * depth, 128)
+    place = pl.ds(pl.multiple_of(shift, 16), depth)
+    staged = [
+        pltpu.make_async_copy(img_feat, feat.at[0], stage.at[0]),
+        pltpu.make_async_copy(txt_feat, feat.at[1], stage.at[1]),
+        pltpu.make_async_copy(w_img, weight.at[0, place], stage.at[2]),
+        pltpu.make_async_copy(w_txt, weight.at[1, place], stage.at[3]),
+        pltpu.make_async_copy(pair, own_index, stage.at[4]),
+        pltpu.make_async_copy(log_scale, own_scale, stage.at[5]),
+        pltpu.make_async_copy(bias, own_bias, stage.at[6]),
+    ]
+    for c in staged:
+        c.start()
+    if spare:
+        empty = pl.ds(pl.multiple_of(depth * (1 - lax.div(shift, spare)), 16), spare)
+        weight[:, empty] = jnp.zeros((2, spare, columns), jnp.bfloat16)
+    for c in staged:
+        c.wait()
+    pl.semaphore_wait(barrier, cycle + group - 2)
+
+    def columns_of(device):
+        start = lax.div(device * depth, 128) * 128
+        return feat.at[:, :, pl.ds(pl.multiple_of(start, 128), width)]
+
+    sends = []
+    for d in range(1, cycle):
+        c = copy(columns_of(ahead(d)), feats.at[here], feat_send.at[d], feat_recv.at[d], (ahead(d), member))
+        c.start()
+        sends.append(c)
+
     lane = lax.broadcasted_iota(jnp.int32, (rows, total), 1)
     row = lax.broadcasted_iota(jnp.int32, (rows, total), 0)
-    own_pair = jnp.broadcast_to(pair[...], (rows, total))
-    spread = jnp.where(lane - here * rows == row, own_pair.astype(jnp.float32), 0.0)
-    pairs[here] = jnp.broadcast_to(jnp.sum(spread, axis=0, keepdims=True), (8, total))
-    pl.semaphore_wait(barrier, cycle + group - 2)
-
-    sends = []
-    for d in range(1, cycle):
-        c = copy(feat.at[ahead(d)], feats.at[here], feat_send.at[d], feat_recv.at[d], (ahead(d), member))
-        c.start()
-        sends.append(c)
-    for d in range(1, cycle):
-        c = copy(pairs.at[here], pairs.at[here], pair_send.at[d], pair_recv.at[d], (ahead(d), member))
-        c.start()
-        sends.append(c)
+    square_lane = lax.broadcasted_iota(jnp.int32, (rows, rows), 1)
+    square_row = lax.broadcasted_iota(jnp.int32, (rows, rows), 0)
+    index = jnp.broadcast_to(own_index[...].reshape(1, rows), (rows, rows)).astype(jnp.float32)
+    index = jnp.sum(jnp.where(square_lane == square_row, index, 0.0), axis=1, keepdims=True)
+    mine = lane - here * rows == row
+
+    def spread(column):
+        return jnp.sum(jnp.where(mine, jnp.broadcast_to(column, (rows, total)), 0.0), axis=0, keepdims=True)
 
     def product(block):
         return (
-            jnp.dot(block[:rows], w_img[...], preferred_element_type=jnp.float32),
-            jnp.dot(block[rows:], w_txt[...], preferred_element_type=jnp.float32),
+            jnp.dot(block[0], weight[0], preferred_element_type=jnp.float32),
+            jnp.dot(block[1], weight[1], preferred_element_type=jnp.float32),
         )
 
-    image_sum, text_sum = product(feat[here])
+    image_sum, text_sum = product(columns_of(here)[...])
     for d in range(1, cycle):
         source = behind(d)
-        copy(feat.at[here], feats.at[source], feat_send.at[d], feat_recv.at[d], (source, member)).wait_recv()
+        copy(columns_of(here), feats.at[source], feat_send.at[d], feat_recv.at[d], (source, member)).wait_recv()
         first, second = product(feats[source])
         partial[source, :rows] = first.astype(jnp.bfloat16)
         partial[source, rows:] = second.astype(jnp.bfloat16)
@@ -178,7 +214,13 @@
         image_sum = image_sum + parts[source, :rows].astype(jnp.float32)
         text_sum = text_sum + parts[source, rows:].astype(jnp.float32)
 
-    pre = jnp.concatenate([image_sum, text_sum], axis=0).astype(jnp.bfloat16).astype(jnp.float32)
+    own = jnp.concatenate([image_sum, text_sum], axis=0).astype(jnp.bfloat16)
+    every[here] = own
+    for d in range(1, cycle):
+        c = copy(every.at[here], every.at[here], every_send.at[d], every_recv.at[d], (ahead(d), member))
+        c.start()
+        sends.append(c)
+    pre = own.astype(jnp.float32)
     squares[member] = jnp.broadcast_to(jnp.sum(pre * pre, axis=1, keepdims=True), (2 * rows, 128))
     for e in range(1, group):
         c = copy(squares.at[member], squares.at[member], square_send.at[e], square_recv.at[e], (here, mate(e)))
@@ -191,16 +233,18 @@
     for k in range(1, group):
         square = square + squares[k]
     norm = lax.rsqrt(square + epsilon)[:, :1]
-    own = (pre * norm).astype(jnp.bfloat16)
-    every[here] = own
-    for d in range(1, cycle):
-        c = copy(every.at[here], every.at[here], every_send.at[d], every_recv.at[d], (ahead(d), member))
-        c.start()
-        sends.append(c)
+    kind = lax.broadcasted_iota(jnp.int32, (8, total), 0)
+    norms[here] = jnp.where(
+        kind == 0, spread(norm[:rows]), jnp.where(kind == 1, spread(norm[rows:]), spread(index))
+    )
+    for d in range(1, cycle):
+        c = copy(norms.at[here], norms.at[here], norm_send.at[d], norm_recv.at[d], (ahead(d), member))
+        c.start()
+        sends.append(c)
+
     for d in range(1, cycle):
         source = behind(d)
         copy(every.at[source], every.at[source], every_send.at[d], every_recv.at[d], (source, member)).wait_recv()
-        copy(pairs.at[source], pairs.at[source], pair_send.at[d], pair_recv.at[d], (source, member)).wait_recv()
     images = every[:, :rows].reshape(total, columns)
     texts = every[:, rows:].reshape(total, columns)
     across = (((1,), (1,)), ((), ()))
@@ -210,35 +254,39 @@
         c = copy(scores.at[member], scores.at[member], score_send.at[e], score_recv.at[e], (here, mate(e)))
         c.start()
         sends.append(c)
-    scale = jnp.exp(jnp.full((1, 1), log_scale[0], jnp.float32))
-    offset = bias[0]
-    all_pairs = pairs[0]
+    for d in range(1, cycle):
+        source = behind(d)
+        copy(norms.at[source], norms.at[source], norm_send.at[d], norm_recv.at[d], (source, member)).wait_recv()
+    scale = jnp.exp(own_scale[...].reshape(1, 1))
+    offset = own_bias[...].reshape(1, 1)
+    across_norms = norms[0]
     for k in range(1, cycle):
-        all_pairs = all_pairs + pairs[k]
-    of_texts = jnp.broadcast_to(all_pairs[:1], (rows, total)) == (here * rows + row).astype(jnp.float32)
-    of_images = own_pair == lane
+        across_norms = across_norms + norms[k]
+    image_norm, text_norm, indices = across_norms[0:1], across_norms[1:2], across_norms[2:3]
+    of_texts = jnp.broadcast_to(indices, (rows, total)) == (here * rows + row).astype(jnp.float32)
+    of_images = jnp.broadcast_to(index, (rows, total)) == lane.astype(jnp.float32)
     for e in range(1, group):
         source = mate_behind(e)
         copy(scores.at[source], scores.at[source], score_send.at[e], score_recv.at[e], (here, source)).wait_recv()
     score = scores[0]
     for k in range(1, group):
         score = score + scores[k]
-    text_coef = coefficients(score[rows:], of_texts, scale, offset)
-    text_grad = scale * jnp.dot(text_coef, images, preferred_element_type=jnp.float32)
+    text_coef = coefficients(score[rows:] * (norm[rows:] * image_norm), of_texts, scale, offset)
+    text_grad = scale * weighted(text_coef * image_norm, images)
     for k in range(group):
-        pieces[0, k] = text_grad[k * piece_rows:(k + 1) * piece_rows]
+        pieces[0, k] = text_grad[k * piece_rows : (k + 1) * piece_rows]
     for e in range(1, group):
         c = copy(pieces.at[0, mate(e)], pieces.at[1, member], piece_send.at[e], piece_recv.at[e], (here, mate(e)))
         c.start()
         sends.append(c)
     pieces[1, member] = pieces[0, member]
-    image_coef = coefficients(score[:rows], of_images, scale, offset)
-    image_out[...] = scale * jnp.dot(image_coef, texts, preferred_element_type=jnp.float32)
+    image_coef = coefficients(score[:rows] * (norm[:rows] * text_norm), of_images, scale, offset)
+    image_out[...] = scale * weighted(image_coef * text_norm, texts)
     for e in range(1, group):
         source = mate_behind(e)
         copy(pieces.at[0, source], pieces.at[1, source], piece_send.at[e], piece_recv.at[e], (here, source)).wait_recv()
     for k in range(group):
-        text_out[:, k * columns:(k + 1) * columns] = pieces[1, k]
+        text_out[:, k * columns : (k + 1) * columns] = pieces[1, k]
     for c in sends:
         c.wait_send()
 
@@ -246,13 +294,12 @@
 def full_window(img_feat, txt_feat, w_img, w_txt, pair_index, log_scale, bias):
     cycle = lax.axis_size("batch")
     group = lax.axis_size("mp")
-    rows = img_feat.shape[0]
+    rows, features = img_feat.shape
     depth, columns = w_img.shape
     total = cycle * rows
-    feat = jnp.concatenate([img_feat, txt_feat], axis=0)
-    feat = feat.reshape(2 * rows, cycle, depth).transpose(1, 0, 2)
+    width = cover(depth)
     vmem = pl.BlockSpec(memory_space=pltpu.VMEM)
-    smem = pl.BlockSpec(memory_space=pltpu.SMEM)
+    anywhere = pl.BlockSpec(memory_space=pl.ANY)
     batch_sems = [pltpu.SemaphoreType.DMA((cycle,))] * 2
     group_sems = [pltpu.SemaphoreType.DMA((group,))] * 2
     return pl.pallas_call(
@@ -261,10 +308,15 @@
             jax.ShapeDtypeStruct((rows, columns), jnp.float32),
             jax.ShapeDtypeStruct((rows // group, group * columns), jnp.float32),
         ),
-        in_specs=[vmem, vmem, vmem, vmem, smem, smem],
+        in_specs=[anywhere] * 7,
         out_specs=(vmem, vmem),
         scratch_shapes=[
-            pltpu.VMEM((cycle, 2 * rows, depth), jnp.bfloat16),
+            pltpu.VMEM((2, rows, features), jnp.bfloat16),
+            pltpu.VMEM((2, width, columns), jnp.bfloat16),
+            pltpu.VMEM((rows,), jnp.int32),
+            pltpu.VMEM((1,), jnp.float32),
+            pltpu.VMEM((1,), jnp.float32),
+            pltpu.VMEM((cycle, 2, rows, width), jnp.bfloat16),
             pltpu.VMEM((cycle, 2 * rows, columns), jnp.bfloat16),
             pltpu.VMEM((cycle, 2 * rows, columns), jnp.bfloat16),
             pltpu.VMEM((cycle, 2 * rows, columns), jnp.bfloat16),
@@ -272,18 +324,26 @@
             pltpu.VMEM((group, 2 * rows, total), jnp.float32),
             pltpu.VMEM((cycle, 8, total), jnp.float32),
             pltpu.VMEM((2, group, rows // group, columns), jnp.float32),
+            pltpu.SemaphoreType.DMA((7,)),
         ]
-        + batch_sems * 3
-        + group_sems * 2
-        + batch_sems
-        + group_sems,
+        + batch_sems * 4
+        + group_sems * 3,
         compiler_params=pltpu.CompilerParams(collective_id=0, has_side_effects=True),
-    )(feat, w_img, w_txt, pair_index.reshape(rows, 1), log_scale, bias)
+    )(img_feat, txt_feat, w_img, w_txt, pair_index, log_scale, bias)
+
+
+def fits_one_kernel(cycle, rows, features, depth):
+    width = cover(depth)
+    for device in range(cycle):
+        shift = device * depth % 128
+        if shift not in (0, width - depth) or device * depth - shift + width > features:
+            return False
+    return min(cycle, 32) == cycle and rows % 16 == 0 and depth % 16 == 0
 
 
 def local(*operands):
     cycle = lax.axis_size("batch")
-    if min(cycle, 32) == cycle:
+    if fits_one_kernel(cycle, *operands[0].shape, operands[2].shape[0]):
         return full_window(*operands)
     return windowed(*operands)
 

time: 39.8 us -> 33 us (0.83)
  Pallas kernels: 32.3 us -> 28.9 us
  local copies, waits for them, and re-layouts: 4.12 us -> 1.96 us
  other arithmetic: 0.83 us -> 0 us
    pallas_call x1, Pallas kernels: 32.3 us -> 28.9 us  [full_window(): pl.pallas_call(functools.partial(full_window_kernel, cycle, group), out_s...]
    reshape x3 -> x0, local copies, waits for them, and re-layouts: 1.51 us -> none  [the longest x2 0.83 us: full_window(): feat = feat.reshape(2 * rows, cycle, depth).transpose(1, 0, 2)]
    concatenate x1 -> x0, other arithmetic: 0.83 us -> none  [full_window(): feat = jnp.concatenate([img_feat, txt_feat], axis=0)]
    unnamed x6 -> x4, local copies, waits for them, and re-layouts: 2.62 us -> 1.96 us
where the time goes in v2:
time: 33 us; the launch traced here: 32.8 us
  Pallas kernels  28.9 us (88%)
  local copies, waits for them, and re-layouts  1.96 us (6%)
  between operations  1.94 us (6%)
    pallas_call x1, Pallas kernels, full_window(): pl.pallas_call(functools.partial(full_window_kernel, cycle, group), out_s...  28.9 us
    unnamed x4, local copies, waits for them, and re-layouts  1.96 us

profile of v2, /device:TPU:0, one launch (start us, length us, event | category | flops | bytes accessed | tf_op | source)
XLA Modules:
  0.0 32.8 jit_solution(15745142310109996518)
XLA Ops:
  1.9 28.9 %shard_map.86 = (f32[16,288]{1,0:T(8,128)}, f32[4,1152]{1,0:T(4,128)}) custom-call(bf16[16,1536]{1,0:T(8,128)(2,1)} %img_feat.1, bf16[16,1536]{1,0:T(8,128)(2,1)} %txt_feat.1, bf16[192,288]{1,0:T(8,128)(2,1)} %w_img.1, bf16[192,288]{1,0:T(8,128)(2,1)} %w_txt.1, s32[16]{0:T(128)} %pair.1, f32[1]{0:T(128)S(6)} %copy.11.log_scale, f32[1]{0:T(128)S(6)} %copy.12.bias), custom_call_target="tpu_custom_call" | custom-call | tf_op jit(solution)/shard_map/pallas_call | solution.py:305
  30.8 0.0 copy-start
  30.8 1.4 %copy.13 = f32[16,288]{1,0:T(8,128)} copy(f32[16,288]{1,0:T(8,128)} %get-tuple-element.4) | data formatting | bytes 36864
  32.2 0.0 copy-done
  32.2 0.6 %copy.14 = f32[4,1152]{1,0:T(4,128)} copy(f32[4,1152]{1,0:T(4,128)S(1)} %copy-done) | data formatting | bytes 36864
Async XLA Ops:
  30.8 1.4 %copy-start = (f32[4,1152]{1,0:T(4,128)S(1)}, f32[4,1152]{1,0:T(4,128)}, u32[]{:S(2)}) copy-start(f32[4,1152]{1,0:T(4,128)} %get-tuple-element.5) | copy-start | bytes 55300

commit v3 on v0

--- a/solution.py
+++ b/solution.py
@@ -1,6 +1,10 @@
+import functools
+
 import jax
 import jax.numpy as jnp
 from jax import lax
+from jax.experimental import pallas as pl
+from jax.experimental.pallas import tpu as pltpu
 from jax.sharding import PartitionSpec as P
 
 epsilon = 1e-06
@@ -34,7 +38,7 @@
     return (image_term, text_term)
 
 
-def local(img_feat, txt_feat, w_img, w_txt, pair_index, log_scale, bias):
+def windowed(img_feat, txt_feat, w_img, w_txt, pair_index, log_scale, bias):
     rows = img_feat.shape[0]
     cycle_size = lax.axis_size("batch")
     group_size = lax.axis_size("mp")
@@ -86,6 +90,308 @@
     text_total = from_behind(grads, "batch", -half)
     image_part = lax.psum_scatter(image_total, "mp", scatter_dimension=1, tiled=True)
     return (scale * image_part, scale * text_total)
+
+
+MESH = pl.DeviceIdType.MESH
+
+
+def coefficients(scores, matched, scale, offset):
+    label = jnp.where(matched, 1.0, -1.0).astype(jnp.float32)
+    logits = scale * scores + offset
+    return (-label * jax.nn.sigmoid(-label * logits)).astype(jnp.bfloat16).astype(jnp.float32)
+
+
+def weighted(coef, block):
+    high = coef.astype(jnp.bfloat16)
+    low = (coef - high.astype(jnp.float32)).astype(jnp.bfloat16)
+    both = jnp.dot(jnp.concatenate([high, low], axis=0), block, preferred_element_type=jnp.float32)
+    return both[: coef.shape[0]] + both[coef.shape[0] :]
+
+
+def full_window_kernel(
+    lines, group, img_feat, txt_feat, w_img, w_txt, pair, log_scale, bias, image_out, text_out,
+    feat, loaded, own_index, own_scale, own_bias, weight, feats, products, partial, parts, kept, others,
+    squares, scores, norms, pairs, halves, pieces, texts,
+    stage, feat_send, feat_recv, weight_sem, pair_sem, part_send, part_recv, other_send, other_recv,
+    norm_send, norm_recv, square_send, square_recv, score_send, score_recv, half_sem, piece_send, piece_recv,
+):
+    here = lax.axis_index("batch")
+    member = lax.axis_index("mp")
+    line = lax.div(here, 2)
+    side = lax.rem(here, 2)
+    rows = img_feat.shape[0]
+    both = 2 * rows
+    total = lines * both
+    depth, columns = w_img.shape
+    width = 2 * depth
+    piece_rows = rows // group
+
+    def ahead(d):
+        return lax.rem(line + d, lines)
+
+    def behind(d):
+        return lax.rem(line + lines - d, lines)
+
+    def mate(e):
+        return lax.rem(member + e, group)
+
+    def mate_behind(e):
+        return lax.rem(member + group - e, group)
+
+    def side_of(flip):
+        return 1 - side if flip else side
+
+    def copy(src, dst, send, recv, device):
+        return pltpu.make_async_remote_copy(
+            src_ref=src, dst_ref=dst, send_sem=send, recv_sem=recv,
+            device_id=device, device_id_type=MESH,
+        )
+
+    neighbour = (2 * line + 1 - side, member)
+    barrier = pltpu.get_barrier_semaphore()
+    hops = [(d, flip) for d in range(lines) for flip in (0, 1) if d or flip]
+    for d, flip in hops:
+        pl.semaphore_signal(
+            barrier, inc=1, device_id=(2 * ahead(d) + side_of(flip), member), device_id_type=MESH
+        )
+    for e in range(1, group):
+        for flip in (0, 1):
+            pl.semaphore_signal(
+                barrier, inc=1, device_id=(2 * line + side_of(flip), mate(e)), device_id_type=MESH
+            )
+
+    staged = [
+        pltpu.make_async_copy(img_feat, feat.at[0], stage.at[0]),
+        pltpu.make_async_copy(txt_feat, feat.at[1], stage.at[1]),
+        pltpu.make_async_copy(w_img, loaded.at[0], stage.at[2]),
+        pltpu.make_async_copy(w_txt, loaded.at[1], stage.at[3]),
+        pltpu.make_async_copy(pair, own_index, stage.at[4]),
+        pltpu.make_async_copy(log_scale, own_scale, stage.at[5]),
+        pltpu.make_async_copy(bias, own_bias, stage.at[6]),
+    ]
+    for c in staged:
+        c.start()
+    for c in staged:
+        c.wait()
+    square_lane = lax.broadcasted_iota(jnp.int32, (rows, rows), 1)
+    square_row = lax.broadcasted_iota(jnp.int32, (rows, rows), 0)
+    index = jnp.broadcast_to(own_index[...].reshape(1, rows), (rows, rows)).astype(jnp.float32)
+    index = jnp.sum(jnp.where(square_lane == square_row, index, 0.0), axis=1, keepdims=True)
+    pairs[side] = jnp.broadcast_to(index, (rows, total))
+    pl.semaphore_wait(barrier, len(hops) + 2 * (group - 1))
+
+    sends = []
+
+    def send(*how):
+        c = copy(*how)
+        c.start()
+        sends.append(c)
+
+    def slab(tower, of_line):
+        return feat.at[tower, :, pl.ds(pl.multiple_of(of_line * width, 128), width)]
+
+    for d, flip in hops:
+        to = 2 * ahead(d) + side_of(flip)
+        k = 2 * d + flip
+        send(slab(side_of(flip), ahead(d)), feats.at[here], feat_send.at[k], feat_recv.at[k], (to, member))
+    send(loaded.at[1 - side], weight.at[side], weight_sem.at[0], weight_sem.at[1], neighbour)
+    send(pairs.at[side], pairs.at[side], pair_sem.at[0], pair_sem.at[1], neighbour)
+    feats[here] = slab(side, line)[...]
+    weight[side] = loaded[side]
+    for d, flip in hops:
+        source = 2 * behind(d) + side_of(flip)
+        k = 2 * d + flip
+        copy(slab(side, line), feats.at[source], feat_send.at[k], feat_recv.at[k], (source, member)).wait_recv()
+    copy(
+        loaded.at[side], weight.at[1 - side], weight_sem.at[0], weight_sem.at[1], neighbour
+    ).wait_recv()
+    product = jnp.dot(
+        feats[...].reshape(total, width), weight[...].reshape(width, columns), preferred_element_type=jnp.float32
+    )
+    products[...] = product.reshape(lines, both, columns)
+    partial[...] = product.reshape(lines, both, columns).astype(jnp.bfloat16)
+    for d in range(1, lines):
+        send(
+            partial.at[ahead(d)], parts.at[line], part_send.at[d], part_recv.at[d], (2 * ahead(d) + side, member)
+        )
+    summed = products[line]
+    for d in range(1, lines):
+        source = behind(d)
+        copy(
+            partial.at[source], parts.at[source], part_send.at[d], part_recv.at[d], (2 * source + side, member)
+        ).wait_recv()
+        summed = summed + parts[source].astype(jnp.float32)
+
+    own = summed.astype(jnp.bfloat16)
+    kept[...] = own
+    for d in range(lines):
+        send(kept, others.at[line], other_send.at[d], other_recv.at[d], (2 * ahead(d) + 1 - side, member))
+    pre = own.astype(jnp.float32)
+    squares[member] = jnp.broadcast_to(jnp.sum(pre * pre, axis=1, keepdims=True), (both, 128))
+    for e in range(1, group):
+        send(squares.at[member], squares.at[member], square_send.at[e], square_recv.at[e], (here, mate(e)))
+    copy(pairs.at[1 - side], pairs.at[1 - side], pair_sem.at[0], pair_sem.at[1], neighbour).wait_recv()
+    lane = lax.broadcasted_iota(jnp.int32, (both, total), 1)
+    row = lax.broadcasted_iota(jnp.int32, (both, total), 0) + line * both
+    wanted = pairs[...].reshape(both, total)
+
+    def spread(block):
+        return jnp.sum(jnp.where(lane == row, block, 0.0), axis=0, keepdims=True)
+
+    wanted_row = spread(wanted)
+    for e in range(1, group):
+        source = mate_behind(e)
+        copy(squares.at[source], squares.at[source], square_send.at[e], square_recv.at[e], (here, source)).wait_recv()
+    square = squares[0]
+    for k in range(1, group):
+        square = square + squares[k]
+    norm = lax.rsqrt(square + epsilon)[:, :1]
+    kind = lax.broadcasted_iota(jnp.int32, (8, total), 0)
+    norm_out = norms.at[lines]
+    norm_out[...] = jnp.where(kind == 0, spread(jnp.broadcast_to(norm, (both, total))), wanted_row)
+    for d in range(lines):
+        send(norm_out, norms.at[line], norm_send.at[d], norm_recv.at[d], (2 * ahead(d) + 1 - side, member))
+
+    for d in range(lines):
+        source = behind(d)
+        copy(
+            kept, others.at[source], other_send.at[d], other_recv.at[d], (2 * source + 1 - side, member)
+        ).wait_recv()
+    block = others[...].reshape(total, columns)
+    scores[member] = lax.dot_general(own, block, (((1,), (1,)), ((), ())), preferred_element_type=jnp.float32)
+    for e in range(1, group):
+        send(scores.at[member], scores.at[member], score_send.at[e], score_recv.at[e], (here, mate(e)))
+    for d in range(lines):
+        source = behind(d)
+        copy(
+            norm_out, norms.at[source], norm_send.at[d], norm_recv.at[d], (2 * source + 1 - side, member)
+        ).wait_recv()
+    scale = jnp.exp(own_scale[...].reshape(1, 1))
+    offset = own_bias[...].reshape(1, 1)
+    gathered = norms[0]
+    for k in range(1, lines):
+        gathered = gathered + norms[k]
+    other_norm = gathered[0:1]
+    left = jnp.where(side == 0, wanted, row.astype(jnp.float32))
+    right = jnp.where(side == 0, lane.astype(jnp.float32), jnp.broadcast_to(gathered[1:2], (both, total)))
+    matched = left == right
+    factor = norm * other_norm
+    for e in range(1, group):
+        source = mate_behind(e)
+        copy(scores.at[source], scores.at[source], score_send.at[e], score_recv.at[e], (here, source)).wait_recv()
+    score = scores[0]
+    for k in range(1, group):
+        score = score + scores[k]
+    coef = coefficients(score * factor, matched, scale, offset)
+    grad = scale * weighted(coef * other_norm, block)
+
+    half = copy(halves.at[1], halves.at[2], half_sem.at[0], half_sem.at[1], neighbour)
+    spots = [(e, flip) for e in range(group) for flip in (0, 1) if e or flip]
+
+    def piece(e, flip):
+        return copy(
+            pieces.at[side_of(flip), mate(e)], texts.at[member],
+            piece_send.at[2 * e + flip], piece_recv.at[2 * e + flip],
+            (2 * line + side_of(flip), mate(e)),
+        )
+
+    def arrived(e, flip):
+        source = mate_behind(e)
+        copy(
+            pieces.at[side, source], texts.at[source],
+            piece_send.at[2 * e + flip], piece_recv.at[2 * e + flip],
+            (2 * line + side_of(flip), source),
+        ).wait_recv()
+
+    @pl.when(side == 0)
+    def _():
+        halves[1] = grad[rows:]
+        half.start()
+        image_out[...] = grad[:rows]
+        for e in range(group):
+            arrived(e, 1)
+        half.wait_send()
+
+    @pl.when(side == 1)
+    def _():
+        for k in range(2 * group):
+            pieces[k // group, k % group] = grad[k * piece_rows : (k + 1) * piece_rows]
+        for e, flip in spots:
+            piece(e, flip).start()
+        texts[member] = pieces[side, member]
+        half.wait_recv()
+        image_out[...] = halves[2]
+        for e in range(1, group):
+            arrived(e, 0)
+        for e, flip in spots:
+            piece(e, flip).wait_send()
+
+    for k in range(group):
+        text_out[:, k * columns : (k + 1) * columns] = texts[k]
+    for c in sends:
+        c.wait_send()
+
+
+def full_window(img_feat, txt_feat, w_img, w_txt, pair_index, log_scale, bias):
+    lines = lax.axis_size("batch") // 2
+    group = lax.axis_size("mp")
+    rows, features = img_feat.shape
+    depth, columns = w_img.shape
+    total = 2 * lines * rows
+    vmem = pl.BlockSpec(memory_space=pltpu.VMEM)
+    anywhere = pl.BlockSpec(memory_space=pl.ANY)
+
+    def sems(count):
+        return pltpu.SemaphoreType.DMA((count,))
+
+    return pl.pallas_call(
+        functools.partial(full_window_kernel, lines, group),
+        out_shape=(
+            jax.ShapeDtypeStruct((rows, columns), jnp.float32),
+            jax.ShapeDtypeStruct((rows // group, group * columns), jnp.float32),
+        ),
+        in_specs=[anywhere] * 7,
+        out_specs=(vmem, vmem),
+        scratch_shapes=[
+            pltpu.VMEM((2, rows, features), jnp.bfloat16),
+            pltpu.VMEM((2, depth, columns), jnp.bfloat16),
+            pltpu.VMEM((rows,), jnp.int32),
+            pltpu.VMEM((1,), jnp.float32),
+            pltpu.VMEM((1,), jnp.float32),
+            pltpu.VMEM((2, depth, columns), jnp.bfloat16),
+            pltpu.VMEM((2 * lines, rows, 2 * depth), jnp.bfloat16),
+            pltpu.VMEM((lines, 2 * rows, columns), jnp.float32),
+            pltpu.VMEM((lines, 2 * rows, columns), jnp.bfloat16),
+            pltpu.VMEM((lines, 2 * rows, columns), jnp.bfloat16),
+            pltpu.VMEM((2 * rows, columns), jnp.bfloat16),
+            pltpu.VMEM((lines, 2 * rows, columns), jnp.bfloat16),
+            pltpu.VMEM((group, 2 * rows, 128), jnp.float32),
+            pltpu.VMEM((group, 2 * rows, total), jnp.float32),
+            pltpu.VMEM((lines + 1, 8, total), jnp.float32),
+            pltpu.VMEM((2, rows, total), jnp.float32),
+            pltpu.VMEM((3, rows, columns), jnp.float32),
+            pltpu.VMEM((2, group, rows // group, columns), jnp.float32),
+            pltpu.VMEM((group, rows // group, columns), jnp.float32),
+        ]
+        + [sems(7), sems(2 * lines), sems(2 * lines), sems(2), sems(2)]
+        + [sems(lines)] * 6
+        + [sems(group)] * 4
+        + [sems(2), sems(2 * group), sems(2 * group)],
+        compiler_params=pltpu.CompilerParams(collective_id=0, has_side_effects=True),
+    )(img_feat, txt_feat, w_img, w_txt, pair_index, log_scale, bias)
+
+
+def fits_one_kernel(cycle, group, rows, depth):
+    aligned = rows % 16 == 0 and rows % group == 0 and 2 * depth % 128 == 0
+    return cycle % 2 == 0 and min(cycle, 32) == cycle and aligned
+
+
+def local(*operands):
+    cycle = lax.axis_size("batch")
+    group = lax.axis_size("mp")
+    if fits_one_kernel(cycle, group, operands[0].shape[0], operands[2].shape[0]):
+        return full_window(*operands)
+    return windowed(*operands)
 
 
 def solution(mesh):

time: 182 us -> 31.9 us (0.18)
  blocking collectives: 81.2 us -> 0 us
  waiting for transfers between devices: 71.1 us -> 0 us
  Pallas kernels: 0 us -> 27.8 us
  between operations: 14.8 us -> 1.94 us
  matrix products: 9.47 us -> 0 us
    all_gather x4 -> x0, blocking collectives: 81.2 us -> none  [the longest x1 35.7 us: local(): lax.all_gather(w_txt, 'batch', axis=0, tiled=True)]
    ppermute x18 -> x0, waiting for transfers between devices: 53.4 us -> none  [from_behind(): return lax.ppermute(value, axis, pairs)]
    pallas_call x0 -> x1, Pallas kernels: none -> 27.8 us  [full_window(): pl.pallas_call(functools.partial(full_window_kernel, lines, group), out_s...]
    unnamed x2 -> x0, waiting for transfers between devices: 17.7 us -> none
    dot_general x26 -> x0, matrix products: 9.47 us -> none  [the longest x8 6.23 us: block_update(): lax.dot_general(image, text, (((1,), (1,)), ((), ())), preferred_element_...]
  transfers between devices with their start and end apart: 19 -> 0, of which waited for: 18 -> 0; matrix products, arithmetic and copies ran while one was open for 6% -> 0% of each run, Pallas kernels for 0% -> 0%
where the time goes in v3:
time: 31.9 us; the launch traced here: 31.7 us
  Pallas kernels  27.8 us (87%)
  local copies, waits for them, and re-layouts  1.96 us (6%)
  between operations  1.94 us (6%)
    pallas_call x1, Pallas kernels, full_window(): pl.pallas_call(functools.partial(full_window_kernel, lines, group), out_s...  27.8 us
    unnamed x4, local copies, waits for them, and re-layouts  1.96 us

profile of v3, /device:TPU:0, one launch (start us, length us, event | category | flops | bytes accessed | tf_op | source)
XLA Modules:
  0.0 31.7 jit_solution(16760126552234802009)
XLA Ops:
  1.9 27.8 %shard_map.86 = (f32[16,288]{1,0:T(8,128)}, f32[4,1152]{1,0:T(4,128)}) custom-call(bf16[16,1536]{1,0:T(8,128)(2,1)} %img_feat.1, bf16[16,1536]{1,0:T(8,128)(2,1)} %txt_feat.1, bf16[192,288]{1,0:T(8,128)(2,1)} %w_img.1, bf16[192,288]{1,0:T(8,128)(2,1)} %w_txt.1, s32[16]{0:T(128)} %pair.1, f32[1]{0:T(128)S(6)} %copy.11.log_scale, f32[1]{0:T(128)S(6)} %copy.12.bias), custom_call_target="tpu_custom_call" | custom-call | tf_op jit(solution)/shard_map/pallas_call | solution.py:347
  29.7 0.0 copy-start
  29.7 1.4 %copy.13 = f32[16,288]{1,0:T(8,128)} copy(f32[16,288]{1,0:T(8,128)} %get-tuple-element.4) | data formatting | bytes 36864
  31.0 0.0 copy-done
  31.1 0.6 %copy.14 = f32[4,1152]{1,0:T(4,128)} copy(f32[4,1152]{1,0:T(4,128)S(1)} %copy-done) | data formatting | bytes 36864
Async XLA Ops:
  29.7 1.4 %copy-start = (f32[4,1152]{1,0:T(4,128)S(1)}, f32[4,1152]{1,0:T(4,128)}, u32[]{:S(2)}) copy-start(f32[4,1152]{1,0:T(4,128)} %get-tuple-element.5) | copy-start | bytes 55300

commit v4 on v3

--- a/solution.py
+++ b/solution.py
@@ -137,6 +137,13 @@
 
     def mate_behind(e):
         return lax.rem(member + group - e, group)
+
+    def distant(k):
+        low = k + jnp.where(k >= line, 1, 0)
+        high = lines - 1 - k
+        high = high - jnp.where(high <= line, 1, 0)
+        to = jnp.where(2 * line >= lines, low, high)
+        return to, lax.rem(to + lines - line, lines)
 
     def side_of(flip):
         return 1 - side if flip else side
@@ -190,11 +197,16 @@
     def slab(tower, of_line):
         return feat.at[tower, :, pl.ds(pl.multiple_of(of_line * width, 128), width)]
 
-    for d, flip in hops:
-        to = 2 * ahead(d) + side_of(flip)
-        k = 2 * d + flip
-        send(slab(side_of(flip), ahead(d)), feats.at[here], feat_send.at[k], feat_recv.at[k], (to, member))
     send(loaded.at[1 - side], weight.at[side], weight_sem.at[0], weight_sem.at[1], neighbour)
+    for step in range(lines - 1):
+        to, d = distant(step)
+        for flip in (1, 0):
+            k = 2 * d + flip
+            send(
+                slab(side_of(flip), to), feats.at[here], feat_send.at[k], feat_recv.at[k],
+                (2 * to + side_of(flip), member),
+            )
+    send(slab(1 - side, line), feats.at[here], feat_send.at[1], feat_recv.at[1], neighbour)
     send(pairs.at[side], pairs.at[side], pair_sem.at[0], pair_sem.at[1], neighbour)
     feats[here] = slab(side, line)[...]
     weight[side] = loaded[side]
@@ -210,10 +222,9 @@
     )
     products[...] = product.reshape(lines, both, columns)
     partial[...] = product.reshape(lines, both, columns).astype(jnp.bfloat16)
-    for d in range(1, lines):
-        send(
-            partial.at[ahead(d)], parts.at[line], part_send.at[d], part_recv.at[d], (2 * ahead(d) + side, member)
-        )
+    for step in range(lines - 1):
+        to, d = distant(step)
+        send(partial.at[to], parts.at[line], part_send.at[d], part_recv.at[d], (2 * to + side, member))
     summed = products[line]
     for d in range(1, lines):
         source = behind(d)
@@ -224,8 +235,10 @@
 
     own = summed.astype(jnp.bfloat16)
     kept[...] = own
-    for d in range(lines):
-        send(kept, others.at[line], other_send.at[d], other_recv.at[d], (2 * ahead(d) + 1 - side, member))
+    for step in range(lines - 1):
+        to, d = distant(step)
+        send(kept, others.at[line], other_send.at[d], other_recv.at[d], (2 * to + 1 - side, member))
+    send(kept, others.at[line], other_send.at[0], other_recv.at[0], neighbour)
     pre = own.astype(jnp.float32)
     squares[member] = jnp.broadcast_to(jnp.sum(pre * pre, axis=1, keepdims=True), (both, 128))
     for e in range(1, group):
@@ -347,8 +360,8 @@
     return pl.pallas_call(
         functools.partial(full_window_kernel, lines, group),
         out_shape=(
-            jax.ShapeDtypeStruct((rows, columns), jnp.float32),
-            jax.ShapeDtypeStruct((rows // group, group * columns), jnp.float32),
+            pltpu.VMEM((rows, columns), jnp.float32),
+            pltpu.VMEM((rows // group, group * columns), jnp.float32),
         ),
         in_specs=[anywhere] * 7,
         out_specs=(vmem, vmem),

time: 31.9 us -> 29.9 us (0.937)
  Pallas kernels: 27.8 us -> 26.6 us
  local copies, waits for them, and re-layouts: 1.96 us -> 1.22 us
    pallas_call x1, Pallas kernels: 27.8 us -> 26.6 us  [full_window(): pl.pallas_call(functools.partial(full_window_kernel, lines, group), out_s...]
    unnamed x4 -> x2, local copies, waits for them, and re-layouts: 1.96 us -> 1.22 us
where the time goes in v4:
time: 29.9 us; the launch traced here: 29.8 us
  Pallas kernels  26.6 us (89%)
  between operations  1.93 us (6%)
  local copies, waits for them, and re-layouts  1.22 us (4%)
    pallas_call x1, Pallas kernels, full_window(): pl.pallas_call(functools.partial(full_window_kernel, lines, group), out_s...  26.6 us
    unnamed x2, local copies, waits for them, and re-layouts  1.22 us

profile of v4, /device:TPU:0, one launch (start us, length us, event | category | flops | bytes accessed | tf_op | source)
XLA Modules:
  0.0 29.8 jit_solution(3477033536941296595)
XLA Ops:
  1.9 26.6 %shard_map.86 = (f32[16,288]{1,0:T(8,128)S(1)}, f32[4,1152]{1,0:T(4,128)S(1)}) custom-call(bf16[16,1536]{1,0:T(8,128)(2,1)} %img_feat.1, bf16[16,1536]{1,0:T(8,128)(2,1)} %txt_feat.1, bf16[192,288]{1,0:T(8,128)(2,1)} %w_img.1, bf16[192,288]{1,0:T(8,128)(2,1)} %w_txt.1, s32[16]{0:T(128)} %pair.1, f32[1]{0:T(128)S(6)} %copy.13.log_scale, f32[1]{0:T(128)S(6)} %copy.14.bias), custom_call_target="tpu_custom_call" | custom-call | tf_op jit(solution)/shard_map/pallas_call | solution.py:360
  28.6 0.6 %copy.11 = f32[16,288]{1,0:T(8,128)} copy(f32[16,288]{1,0:T(8,128)S(1)} %get-tuple-element.2) | data formatting | bytes 36864
  29.2 0.6 %copy.12 = f32[4,1152]{1,0:T(4,128)} copy(f32[4,1152]{1,0:T(4,128)S(1)} %get-tuple-element.3) | data formatting | bytes 36864

commit v5 on v4

--- a/solution.py
+++ b/solution.py
@@ -110,9 +110,9 @@
 
 def full_window_kernel(
     lines, group, img_feat, txt_feat, w_img, w_txt, pair, log_scale, bias, image_out, text_out,
-    feat, loaded, own_index, own_scale, own_bias, weight, feats, products, partial, parts, kept, others,
+    feat, loaded, own_index, own_scale, own_bias, weight, tail, feats, products, partial, parts, kept, others,
     squares, scores, norms, pairs, halves, pieces, texts,
-    stage, feat_send, feat_recv, weight_sem, pair_sem, part_send, part_recv, other_send, other_recv,
+    stage, feat_send, feat_recv, weight_sem, tail_sem, pair_sem, part_send, part_recv, other_send, other_recv,
     norm_send, norm_recv, square_send, square_recv, score_send, score_recv, half_sem, piece_send, piece_recv,
 ):
     here = lax.axis_index("batch")
@@ -185,6 +185,15 @@
     index = jnp.broadcast_to(own_index[...].reshape(1, rows), (rows, rows)).astype(jnp.float32)
     index = jnp.sum(jnp.where(square_lane == square_row, index, 0.0), axis=1, keepdims=True)
     pairs[side] = jnp.broadcast_to(index, (rows, total))
+    whole = columns // 128 * 128
+    rest = columns - whole
+    packs = 128 // rest if rest else 1
+    pack_rows = depth // packs
+    if rest:
+        away = jnp.where(side == 0, loaded[1, :, whole:], loaded[0, :, whole:])
+        tail[side] = jnp.concatenate(
+            [away[k * pack_rows : (k + 1) * pack_rows] for k in range(packs)], axis=1
+        )
     pl.semaphore_wait(barrier, len(hops) + 2 * (group - 1))
 
     sends = []
@@ -197,7 +206,11 @@
     def slab(tower, of_line):
         return feat.at[tower, :, pl.ds(pl.multiple_of(of_line * width, 128), width)]
 
-    send(loaded.at[1 - side], weight.at[side], weight_sem.at[0], weight_sem.at[1], neighbour)
+    send(
+        loaded.at[1 - side, :, :whole], weight.at[side, :, :whole], weight_sem.at[0], weight_sem.at[1], neighbour
+    )
+    if rest:
+        send(tail.at[side], tail.at[side], tail_sem.at[0], tail_sem.at[1], neighbour)
     for step in range(lines - 1):
         to, d = distant(step)
         for flip in (1, 0):
@@ -215,8 +228,13 @@
         k = 2 * d + flip
         copy(slab(side, line), feats.at[source], feat_send.at[k], feat_recv.at[k], (source, member)).wait_recv()
     copy(
-        loaded.at[side], weight.at[1 - side], weight_sem.at[0], weight_sem.at[1], neighbour
+        loaded.at[side, :, :whole], weight.at[1 - side, :, :whole], weight_sem.at[0], weight_sem.at[1], neighbour
     ).wait_recv()
+    if rest:
+        copy(tail.at[1 - side], tail.at[1 - side], tail_sem.at[0], tail_sem.at[1], neighbour).wait_recv()
+        packed = tail[1 - side]
+        for k in range(packs):
+            weight[1 - side, k * pack_rows : (k + 1) * pack_rows, whole:] = packed[:, k * rest : (k + 1) * rest]
     product = jnp.dot(
         feats[...].reshape(total, width), weight[...].reshape(width, columns), preferred_element_type=jnp.float32
     )
@@ -372,6 +390,7 @@
             pltpu.VMEM((1,), jnp.float32),
             pltpu.VMEM((1,), jnp.float32),
             pltpu.VMEM((2, depth, columns), jnp.bfloat16),
+            pltpu.VMEM((2, depth * (columns % 128) // 128, 128) if columns % 128 else (2, 8, 128), jnp.bfloat16),
             pltpu.VMEM((2 * lines, rows, 2 * depth), jnp.bfloat16),
             pltpu.VMEM((lines, 2 * rows, columns), jnp.float32),
             pltpu.VMEM((lines, 2 * rows, columns), jnp.bfloat16),
@@ -386,7 +405,7 @@
             pltpu.VMEM((2, group, rows // group, columns), jnp.float32),
             pltpu.VMEM((group, rows // group, columns), jnp.float32),
         ]
-        + [sems(7), sems(2 * lines), sems(2 * lines), sems(2), sems(2)]
+        + [sems(7), sems(2 * lines), sems(2 * lines), sems(2), sems(2), sems(2)]
         + [sems(lines)] * 6
         + [sems(group)] * 4
         + [sems(2), sems(2 * group), sems(2 * group)],
@@ -394,15 +413,18 @@
     )(img_feat, txt_feat, w_img, w_txt, pair_index, log_scale, bias)
 
 
-def fits_one_kernel(cycle, group, rows, depth):
+def fits_one_kernel(cycle, group, rows, depth, columns):
     aligned = rows % 16 == 0 and rows % group == 0 and 2 * depth % 128 == 0
+    rest = columns % 128
+    if rest and (128 % rest or depth % (128 // rest * 16)):
+        return False
     return cycle % 2 == 0 and min(cycle, 32) == cycle and aligned
 
 
 def local(*operands):
     cycle = lax.axis_size("batch")
     group = lax.axis_size("mp")
-    if fits_one_kernel(cycle, group, operands[0].shape[0], operands[2].shape[0]):
+    if fits_one_kernel(cycle, group, operands[0].shape[0], *operands[2].shape):
         return full_window(*operands)
     return windowed(*operands)
 

time: 29.9 us -> 29.2 us (0.977)
  Pallas kernels: 26.6 us -> 25.9 us
    pallas_call x1, Pallas kernels: 26.6 us -> 25.9 us  [full_window(): pl.pallas_call(functools.partial(full_window_kernel, lines, group), out_s...]
where the time goes in v5:
time: 29.2 us; the launch traced here: 29.1 us
  Pallas kernels  25.9 us (89%)
  between operations  1.93 us (7%)
  local copies, waits for them, and re-layouts  1.22 us (4%)
    pallas_call x1, Pallas kernels, full_window(): pl.pallas_call(functools.partial(full_window_kernel, lines, group), out_s...  25.9 us
    unnamed x2, local copies, waits for them, and re-layouts  1.22 us

profile of v5, /device:TPU:0, one launch (start us, length us, event | category | flops | bytes accessed | tf_op | source)
XLA Modules:
  0.0 29.1 jit_solution(6564026787310558617)
XLA Ops:
  1.9 25.9 %shard_map.86 = (f32[16,288]{1,0:T(8,128)S(1)}, f32[4,1152]{1,0:T(4,128)S(1)}) custom-call(bf16[16,1536]{1,0:T(8,128)(2,1)} %img_feat.1, bf16[16,1536]{1,0:T(8,128)(2,1)} %txt_feat.1, bf16[192,288]{1,0:T(8,128)(2,1)} %w_img.1, bf16[192,288]{1,0:T(8,128)(2,1)} %w_txt.1, s32[16]{0:T(128)} %pair.1, f32[1]{0:T(128)S(6)} %copy.13.log_scale, f32[1]{0:T(128)S(6)} %copy.14.bias), custom_call_target="tpu_custom_call" | custom-call | tf_op jit(solution)/shard_map/pallas_call | solution.py:378
  27.8 0.6 %copy.11 = f32[16,288]{1,0:T(8,128)} copy(f32[16,288]{1,0:T(8,128)S(1)} %get-tuple-element.2) | data formatting | bytes 36864
  28.5 0.6 %copy.12 = f32[4,1152]{1,0:T(4,128)} copy(f32[4,1152]{1,0:T(4,128)S(1)} %get-tuple-element.3) | data formatting | bytes 36864

commit v6 on v5

--- a/solution.py
+++ b/solution.py
@@ -157,10 +157,13 @@
     neighbour = (2 * line + 1 - side, member)
     barrier = pltpu.get_barrier_semaphore()
     hops = [(d, flip) for d in range(lines) for flip in (0, 1) if d or flip]
-    for d, flip in hops:
-        pl.semaphore_signal(
-            barrier, inc=1, device_id=(2 * ahead(d) + side_of(flip), member), device_id_type=MESH
-        )
+    for step in range(lines - 1):
+        to, d = distant(step)
+        for flip in (1, 0):
+            pl.semaphore_signal(
+                barrier, inc=1, device_id=(2 * to + side_of(flip), member), device_id_type=MESH
+            )
+    pl.semaphore_signal(barrier, inc=1, device_id=neighbour, device_id_type=MESH)
     for e in range(1, group):
         for flip in (0, 1):
             pl.semaphore_signal(
@@ -280,8 +283,10 @@
     kind = lax.broadcasted_iota(jnp.int32, (8, total), 0)
     norm_out = norms.at[lines]
     norm_out[...] = jnp.where(kind == 0, spread(jnp.broadcast_to(norm, (both, total))), wanted_row)
-    for d in range(lines):
-        send(norm_out, norms.at[line], norm_send.at[d], norm_recv.at[d], (2 * ahead(d) + 1 - side, member))
+    for step in range(lines - 1):
+        to, d = distant(step)
+        send(norm_out, norms.at[line], norm_send.at[d], norm_recv.at[d], (2 * to + 1 - side, member))
+    send(norm_out, norms.at[line], norm_send.at[0], norm_recv.at[0], neighbour)
 
     for d in range(lines):
         source = behind(d)
@@ -290,7 +295,7 @@
         ).wait_recv()
     block = others[...].reshape(total, columns)
     scores[member] = lax.dot_general(own, block, (((1,), (1,)), ((), ())), preferred_element_type=jnp.float32)
-    for e in range(1, group):
+    for e in sorted(range(1, group), key=lambda e: abs(2 * e - group)):
         send(scores.at[member], scores.at[member], score_send.at[e], score_recv.at[e], (here, mate(e)))
     for d in range(lines):
         source = behind(d)

time: 29.2 us -> 29.2 us (level)
  no operation moved by 1% of the time
where the time goes in v6:
time: 29.2 us; the launch traced here: 29.1 us
  Pallas kernels  25.9 us (89%)
  between operations  1.93 us (7%)
  local copies, waits for them, and re-layouts  1.22 us (4%)
    pallas_call x1, Pallas kernels, full_window(): pl.pallas_call(functools.partial(full_window_kernel, lines, group), out_s...  25.9 us
    unnamed x2, local copies, waits for them, and re-layouts  1.22 us

profile of v6, /device:TPU:0, one launch (start us, length us, event | category | flops | bytes accessed | tf_op | source)
XLA Modules:
  0.0 29.1 jit_solution(7515322838691571026)
XLA Ops:
  1.9 25.9 %shard_map.86 = (f32[16,288]{1,0:T(8,128)S(1)}, f32[4,1152]{1,0:T(4,128)S(1)}) custom-call(bf16[16,1536]{1,0:T(8,128)(2,1)} %img_feat.1, bf16[16,1536]{1,0:T(8,128)(2,1)} %txt_feat.1, bf16[192,288]{1,0:T(8,128)(2,1)} %w_img.1, bf16[192,288]{1,0:T(8,128)(2,1)} %w_txt.1, s32[16]{0:T(128)} %pair.1, f32[1]{0:T(128)S(6)} %copy.13.log_scale, f32[1]{0:T(128)S(6)} %copy.14.bias), custom_call_target="tpu_custom_call" | custom-call | tf_op jit(solution)/shard_map/pallas_call | solution.py:383
  27.8 0.6 %copy.11 = f32[16,288]{1,0:T(8,128)} copy(f32[16,288]{1,0:T(8,128)S(1)} %get-tuple-element.2) | data formatting | bytes 36864
  28.5 0.6 %copy.12 = f32[4,1152]{1,0:T(4,128)} copy(f32[4,1152]{1,0:T(4,128)S(1)} %get-tuple-element.3) | data formatting | bytes 36864
